TPU v7x, 32 devices: a whole 2x2x4 slice. The times are simulated.
32 devices in a mesh: sym: 4 (over x, core), row: 8 (over z, y).
Axes of the slice: x: 2, y: 2, z: 4, core: 2. Of those that a mesh axis runs over, the one named last changes fastest.
Arguments:
- vectors: float32 [4, 32768, 256], P('sym', 'row'), may hold values from -6 to 6
- reflectors: float32 [4, 32768, 512], P('sym', 'row'), may hold values from -0.5 to 0.5
- factors: float32 [4, 4, 128, 128], P('sym'), may hold values from -0.03125 to 0.03125
- tiles: bfloat16 [4, 16, 512, 512], P('sym', 'row'), may hold values from -0.0029296875 to 0.0029296875
- tile_left: int32 [4, 16], P('sym', 'row'), may hold values from 0 to 7
- tile_right: int32 [4, 16], P('sym', 'row'), may hold values from 0 to 7
- tile_occupied_mask: int32 [4, 16], P('sym', 'row'), may hold values 0 or 1
- channels: int32 [4, 64], P('sym', 'row'), may hold values from 256 to 512
Outputs:
- dipole: float32 [4, 256, 256], P('sym', 'row')
All inputs are finite; a program needn't handle non-finite values. No bound on the sum of `tile_occupied_mask` on one device may be relied on, other than what follows from the above.
Results may differ from a plain program's by a relative error of at most 0.0049.
Values may be sent and summed in bfloat16 or wider, within the bound.
A program may use at most 64 MiB of HBM per device.

v0:
```python
import functools

import jax
import jax.numpy as jnp
from jax import lax
from jax.experimental import pallas as pl
from jax.experimental.pallas import tpu as pltpu
from jax.sharding import PartitionSpec as P

BLOCK = 512
LANES = 128
JOB_ROWS = 256
SKEW = 3
SWAPPED = (1, 3, 5)
EARLY = ((), ((0, 0),), ((1, 0),))
F32 = jnp.float32
BF16 = jnp.bfloat16
MESH = pl.DeviceIdType.MESH


def split(value):
    high = value.astype(BF16)
    return high, (value - high.astype(F32)).astype(BF16)


def contract(first, second, dims):
    high, low = first
    other_high, other_low = second

    def dot(a, b):
        return lax.dot_general(a, b, (dims, ((), ())), preferred_element_type=F32)

    return dot(high, other_high) + (dot(high, other_low) + dot(low, other_high))


ROWS = ((0,), (0,))
PLAIN = ((1,), (0,))
COLUMNS = ((1,), (1,))


def coupled_ranges(first, count):
    if count < 2:
        return []
    half = count // 2
    here = [(first, half, first + half, count - half)]
    return here + coupled_ranges(first, half) + coupled_ranges(first + half, count - half)


def exchanges(n, job):
    strides = [1 << bit for bit in range(n.bit_length() - 1)]
    if job in SWAPPED and len(strides) > 1:
        strides[:2] = strides[1::-1]
    return strides


def kernel(
    n,
    syms,
    x_hbm,
    v_hbm,
    f_hbm,
    tiles_hbm,
    right_ref,
    left_ref,
    occupied_ref,
    channels_ref,
    out_ref,
    x_buf,
    v_buf,
    v_high,
    v_low,
    slots_vmem,
    slots_smem,
    partial,
    landed,
    full,
    t_ref,
    u_high,
    u_low,
    ket_out,
    ket_in,
    bras,
    own,
    dipole_out,
    dipole_in,
    f_ref,
    tiles_ref,
    x_sem,
    v_sem,
    slot_sem,
    operand_sem,
    reduce_send,
    reduce_recv,
    ket_send,
    ket_recv,
    dipole_send,
    dipole_recv,
):
    panels, width, _ = f_ref.shape
    blocks, _, eig = x_buf.shape
    tile_slots = tiles_ref.shape[0]
    halves = eig // LANES
    sym = lax.axis_index("sym")
    me = lax.axis_index("row")
    after = lax.rem(sym + 1, syms)
    before = lax.rem(sym + syms - 1, syms)

    def load(source, target, sems, r):
        return pltpu.make_async_copy(source.at[r], target.at[r], sems.at[r])

    for r in range(blocks):
        load(v_hbm, v_buf, v_sem, r).start()
    for r in range(blocks):
        load(x_hbm, x_buf, x_sem, r).start()

    f_copy = pltpu.make_async_copy(f_hbm, f_ref, operand_sem.at[0])
    f_copy.start()
    tiles_copy = pltpu.make_async_copy(tiles_hbm, tiles_ref, operand_sem.at[1])
    tiles_copy.start()

    barrier = pltpu.get_barrier_semaphore()
    for d in range(1, n):
        pl.semaphore_signal(
            barrier, inc=1, device_id=(sym, lax.rem(me + d, n)), device_id_type=MESH
        )
    for other in (after, before):
        pl.semaphore_signal(barrier, inc=1, device_id=(other, me), device_id_type=MESH)
    pl.semaphore_wait(barrier, n + 1)

    slots_copy = pltpu.make_async_remote_copy(
        src_ref=right_ref,
        dst_ref=slots_vmem,
        send_sem=slot_sem.at[0],
        recv_sem=slot_sem.at[1],
        device_id=(after, me),
        device_id_type=MESH,
    )
    slots_copy.start()

    ranges = coupled_ranges(0, panels)

    def couple(r, sums):
        load(v_hbm, v_buf, v_sem, r).wait()
        high, low = split(v_buf[r])
        v_high[r] = high
        v_low[r] = low
        out = []
        for total, (a, ca, b, cb) in zip(sums, ranges):
            pa = slice(a * width, (a + ca) * width)
            pb = slice(b * width, (b + cb) * width)
            out.append(
                total + contract((high[:, pa], low[:, pa]), (high[:, pb], low[:, pb]), ROWS)
            )
        return tuple(out)

    sums = lax.fori_loop(
        0, blocks, couple, tuple(jnp.zeros((ca * width, cb * width), F32) for _, ca, _, cb in ranges)
    )
    where = {}
    place = 0
    for total, (a, ca, b, cb) in zip(sums, ranges):
        for i in range(ca):
            for j in range(cb):
                where[(a + i, b + j)] = place
                partial[place : place + width, :] = total[
                    i * width : (i + 1) * width, j * width : (j + 1) * width
                ]
                place = place + width
    coupled_rows = place
    total_rows = coupled_rows + panels * eig
    job_rows = max(JOB_ROWS, 8 * n)
    job_count = total_rows // job_rows
    coupled_jobs = coupled_rows // job_rows
    jobs_of_half = (job_count - coupled_jobs) // halves

    copies = {}
    levels = n.bit_length() - 1

    def digit(job, level):
        return lax.rem(me // exchanges(n, job)[level], 2)

    def span_after(job, level, flip=False):
        offset = job * job_rows
        for below in range(level):
            place = digit(job, below)
            if flip and below == level - 1:
                place = 1 - place
            offset = offset + place * (job_rows >> (below + 1))
        return pl.ds(pl.multiple_of(offset, 8), job_rows >> level)

    def landing(job, level):
        piece = job_rows >> (level + 1)
        slot = (job + 1) * job_rows - 2 * piece
        return slice(slot, slot + piece)

    def start(job, phase):
        level = phase if phase < levels else 2 * levels - 1 - phase
        if phase < levels:
            source = partial.at[span_after(job, level + 1, True)]
            target = landed.at[landing(job, level)]
        else:
            source = full.at[span_after(job, level + 1)]
            target = source
        partner = me + (1 - 2 * digit(job, level)) * exchanges(n, job)[level]
        copy = pltpu.make_async_remote_copy(
            src_ref=source,
            dst_ref=target,
            send_sem=reduce_send.at[job, phase],
            recv_sem=reduce_recv.at[job, phase],
            device_id=(sym, partner),
            device_id_type=MESH,
        )
        copy.start()
        copies[(job, phase)] = copy

    def finish(job, phase):
        copies[(job, phase)].wait()
        if phase < levels:
            span = span_after(job, phase + 1)
            target = full if phase == levels - 1 else partial
            target[span, :] = partial[span, :] + landed[landing(job, phase), :]
        if phase + 1 < 2 * levels:
            start(job, phase + 1)

    for job in range(coupled_jobs):
        start(job, 0)

    def project(r, total):
        load(x_hbm, x_buf, x_sem, r).wait()
        return total + contract(split(x_buf[r]), (v_high[r], v_low[r]), ROWS)

    projected = jnp.zeros((eig, panels * width), F32)
    parts = len(EARLY) + 1
    for part in range(parts):
        projected = lax.fori_loop(
            part * blocks // parts, (part + 1) * blocks // parts, project, projected
        )
        if part < parts - 1:
            for job, phase in EARLY[part]:
                finish(job, phase)
    for h in range(halves):
        for k in range(panels):
            at = coupled_rows + (h * panels + k) * LANES
            partial[at : at + LANES, :] = projected[
                h * LANES : (h + 1) * LANES, k * width : (k + 1) * width
            ]
    for job in range(coupled_jobs, job_count):
        start(job, 0)

    slots_copy.wait()
    to_smem = pltpu.make_async_copy(slots_vmem, slots_smem, slot_sem.at[2])
    to_smem.start()

    def transfer_matrix():
        f_copy.wait()
        for k in reversed(range(panels)):
            here = slice(k * width, (k + 1) * width)
            t_ref[here, here] = f_ref[k]
            if k:
                t_ref[here, : k * width] = jnp.zeros((width, k * width), F32)
            if k < panels - 1:
                later = slice((k + 1) * width, panels * width)
                row = jnp.concatenate(
                    [full[where[(k, j)] : where[(k, j)] + width, :] for j in range(k + 1, panels)],
                    axis=1,
                )
                inner = contract(split(row), split(t_ref[later, later]), PLAIN)
                t_ref[here, later] = -contract(split(f_ref[k]), split(inner), PLAIN)

    def update(h):
        begin = coupled_rows + h * panels * LANES
        gathered = jnp.concatenate(
            [full[begin + k * LANES : begin + (k + 1) * LANES, :] for k in range(panels)], axis=1
        )
        high, low = split(contract(split(t_ref[...]), split(gathered), COLUMNS))
        u_high[h] = high
        u_low[h] = low

    def finished(slot, h):
        change = contract((v_high[slot], v_low[slot]), (u_high[h], u_low[h]), PLAIN)
        live = lax.broadcasted_iota(jnp.int32, (BLOCK, LANES), 0) < channels_ref[0, slot]
        value = x_buf[slot, :, h * LANES : (h + 1) * LANES] - change
        return jnp.where(live, value, 0.0)

    kets = {}

    def right_blocks(h):
        for t in range(tile_slots):
            ket_out[h, t] = finished(slots_smem[0, t], h).astype(BF16)
            copy = pltpu.make_async_remote_copy(
                src_ref=ket_out.at[h, t],
                dst_ref=ket_in.at[h, t],
                send_sem=ket_send.at[h, t],
                recv_sem=ket_recv.at[h, t],
                device_id=(before, me),
                device_id_type=MESH,
            )
            copy.start()
            kets[(h, t)] = copy

    def left_blocks(h):
        for t in range(tile_slots):
            occupied = occupied_ref[0, t].astype(F32)
            bras[t, :, h * LANES : (h + 1) * LANES] = (
                finished(left_ref[0, t], h) * occupied
            ).astype(BF16)

    to_smem.wait()
    events = [(job + SKEW * phase, job, phase) for job in range(job_count) for phase in range(2 * levels)]
    early = [event for part in EARLY for event in part]
    for _, job, phase in sorted(events):
        if (job, phase) not in early:
            finish(job, phase)
        if phase == 2 * levels - 1:
            if job == coupled_jobs - 1:
                transfer_matrix()
            done = job + 1 - coupled_jobs
            if done > 0 and done % jobs_of_half == 0:
                h = done // jobs_of_half - 1
                update(h)
                right_blocks(h)
                if h < halves - 1:
                    left_blocks(h)
    left_blocks(halves - 1)

    share = eig // n
    tiles_copy.wait()
    sends = []
    for h in range(halves):
        total = jnp.zeros((eig, LANES), F32)
        for t in range(tile_slots):
            kets[(h, t)].wait()
            product = jnp.dot(tiles_ref[t], ket_in[h, t], preferred_element_type=F32).astype(BF16)
            total = total + lax.dot_general(
                bras[t], product, (ROWS, ((), ())), preferred_element_type=F32
            )
        own[h] = total.reshape(n, share, LANES)
        dipole_out[h] = total.reshape(n, share, LANES).astype(BF16)
        for d in range(1, n):
            target = lax.rem(me + d, n)
            copy = pltpu.make_async_remote_copy(
                src_ref=dipole_out.at[h, target],
                dst_ref=dipole_in.at[h, d - 1],
                send_sem=dipole_send.at[h, d - 1],
                recv_sem=dipole_recv.at[h, d - 1],
                device_id=(sym, target),
                device_id_type=MESH,
            )
            copy.start()
            sends.append((h, d, copy))
    results = [own[h, me] for h in range(halves)]
    for h, d, copy in sends:
        copy.wait()
        results[h] = results[h] + dipole_in[h, d - 1].astype(F32)
    for h in range(halves):
        out_ref[0, :, h * LANES : (h + 1) * LANES] = results[h]


def on_device(
    n,
    syms,
    vectors,
    reflectors,
    factors,
    tiles,
    tile_left,
    tile_right,
    tile_occupied_mask,
    channels,
):
    start = vectors[0]
    panels = reflectors[0]
    rows, eig = start.shape
    count, width, _ = factors.shape[1:]
    tile_slots = tiles.shape[1]
    halves = eig // LANES
    phases = 2 * (n.bit_length() - 1)
    blocks = rows // BLOCK
    coupled_rows = count * (count - 1) // 2 * width
    reduced = coupled_rows + count * eig
    jobs = reduced // max(JOB_ROWS, 8 * n)
    share = eig // n
    dma = pltpu.SemaphoreType.DMA
    vmem = pl.BlockSpec(memory_space=pltpu.VMEM)
    smem = pl.BlockSpec(memory_space=pltpu.SMEM)
    hbm = pl.BlockSpec(memory_space=pl.ANY)
    return pl.pallas_call(
        functools.partial(kernel, n, syms),
        out_shape=jax.ShapeDtypeStruct((1, share, eig), F32),
        in_specs=[hbm, hbm, hbm, hbm, vmem, smem, smem, smem],
        out_specs=vmem,
        scratch_shapes=[
            pltpu.VMEM((blocks, BLOCK, eig), F32),
            pltpu.VMEM((blocks, BLOCK, count * width), F32),
            pltpu.VMEM((blocks, BLOCK, count * width), BF16),
            pltpu.VMEM((blocks, BLOCK, count * width), BF16),
            pltpu.VMEM((1, tile_slots), jnp.int32),
            pltpu.SMEM((1, tile_slots), jnp.int32),
            pltpu.VMEM((reduced, width), F32),
            pltpu.VMEM((reduced, width), F32),
            pltpu.VMEM((reduced, width), F32),
            pltpu.VMEM((count * width, count * width), F32),
            pltpu.VMEM((halves, count * width, LANES), BF16),
            pltpu.VMEM((halves, count * width, LANES), BF16),
            pltpu.VMEM((halves, tile_slots, BLOCK, LANES), BF16),
            pltpu.VMEM((halves, tile_slots, BLOCK, LANES), BF16),
            pltpu.VMEM((tile_slots, BLOCK, eig), BF16),
            pltpu.VMEM((halves, n, share, LANES), F32),
            pltpu.VMEM((halves, n, share, LANES), BF16),
            pltpu.VMEM((halves, n - 1, share, LANES), BF16),
            pltpu.VMEM((count, width, width), F32),
            pltpu.VMEM((tile_slots, BLOCK, BLOCK), BF16),
            dma((blocks,)),
            dma((blocks,)),
            dma((3,)),
            dma((2,)),
            dma((jobs, phases)),
            dma((jobs, phases)),
            dma((halves, tile_slots)),
            dma((halves, tile_slots)),
            dma((halves, n - 1)),
            dma((halves, n - 1)),
        ],
        compiler_params=pltpu.CompilerParams(
            collective_id=0, has_side_effects=True, vmem_limit_bytes=60 * 1024 * 1024
        ),
    )(
        start.reshape(blocks, BLOCK, eig),
        panels.reshape(blocks, BLOCK, count * width),
        factors[0],
        tiles[0],
        tile_right,
        tile_left,
        tile_occupied_mask,
        channels,
    )


def solution(mesh):
    return jax.shard_map(
        functools.partial(on_device, mesh.shape["row"], mesh.shape["sym"]),
        mesh=mesh,
        in_specs=(
            P("sym", "row", None),
            P("sym", "row", None),
            P("sym", None, None, None),
            P("sym", "row", None, None),
            P("sym", "row"),
            P("sym", "row"),
            P("sym", "row"),
            P("sym", "row"),
        ),
        out_specs=P("sym", "row", None),
        check_vma=False,
    )
```

profile of v0, /device:TPU:1, one launch (start us, length us, event | category | flops | bytes accessed | tf_op | source)
XLA Modules:
  0.0 58.1 jit_solution(9246811323659743663)
XLA Ops:
  0.0 56.8 %shard_map.82 = f32[1,32,256]{2,1,0:T(8,128)} custom-call(f32[8,512,256]{2,1,0:T(8,128)} %bitcast.5, f32[8,512,512]{2,1,0:T(8,128)} %bitcast.4, f32[4,128,128]{2,1,0:T(8,128)} %bitcast.7, bf16[2,512,512]{2,1,0:T(8,128)(2,1)} %bitcast.6, s32[1,2]{1,0:T(1,128)} %right_ref.1, s32[1,2]{1,0:T(1,128)} %left_ref.1, s32[1,2]{1,0:T(1,128)} %occupied_ref.1, ...), custom_call_target="tpu_custom_call" | custom-call | tf_op jit(solution)/shard_map/pallas_call | solution.py:387
  56.8 1.4 %copy.10 = f32[1,32,256]{2,1,0:T(8,128)} copy(f32[1,32,256]{2,1,0:T(8,128)} %shard_map.82) | data formatting | bytes 65536
where the time goes:
time: 58.3 us; the launch traced here: 58.1 us
  Pallas kernels  56.8 us (97%)
  local copies, waits for them, and re-layouts  1.38 us (2%)
    pallas_call x1, Pallas kernels, on_device(): pl.pallas_call(functools.partial(kernel, n, syms), out_shape=jax.ShapeDty...  56.8 us
    unnamed x1, local copies, waits for them, and re-layouts  1.38 us

commit v1 on v0

--- a/solution.py
+++ b/solution.py
@@ -9,12 +9,14 @@
 
 BLOCK = 512
 LANES = 128
-JOB_ROWS = 256
-SKEW = 3
-SWAPPED = (1, 3, 5)
-EARLY = ((), ((0, 0),), ((1, 0),))
+PACK = 16
+TOP = 15.0
+MARGIN = 1e-3
+LEAST = 2.0**-100
+MOST = 2.0**100
 F32 = jnp.float32
 BF16 = jnp.bfloat16
+I16 = jnp.int16
 MESH = pl.DeviceIdType.MESH
 
 
@@ -46,11 +48,25 @@
     return here + coupled_ranges(first, half) + coupled_ranges(first + half, count - half)
 
 
-def exchanges(n, job):
-    strides = [1 << bit for bit in range(n.bit_length() - 1)]
-    if job in SWAPPED and len(strides) > 1:
-        strides[:2] = strides[1::-1]
-    return strides
+def padded(rows):
+    return -(-rows // PACK) * PACK
+
+
+def encode(value, target):
+    rows = value.shape[0]
+    groups = value.reshape(rows // 8, 8, LANES)
+    peak = jnp.clip(jnp.max(jnp.abs(groups), axis=0), LEAST, MOST)
+    level = jnp.ceil(jnp.log2(peak) + MARGIN) - TOP
+    codes = jnp.round(groups * jnp.exp2(-level)[None])
+    target[:rows, :] = codes.reshape(rows, LANES).astype(jnp.int32).astype(I16)
+    both = jnp.concatenate([level, level], axis=0)
+    target[padded(rows) :, :] = both.astype(jnp.int32).astype(I16)
+
+
+def decode(source, rows):
+    level = source[padded(rows) :, :].astype(jnp.int32).astype(F32)[:8]
+    groups = source[:rows, :].astype(jnp.int32).astype(F32).reshape(rows // 8, 8, LANES)
+    return (groups * jnp.exp2(level)[None]).reshape(rows, LANES)
 
 
 def kernel(
@@ -71,9 +87,15 @@
     v_low,
     slots_vmem,
     slots_smem,
-    partial,
-    landed,
-    full,
+    coupled_part,
+    coupled_out,
+    coupled_in,
+    coupled_all,
+    coupled,
+    inner_part,
+    inner_out,
+    inner_in,
+    inner_all,
     t_ref,
     u_high,
     u_low,
@@ -89,8 +111,10 @@
     v_sem,
     slot_sem,
     operand_sem,
-    reduce_send,
-    reduce_recv,
+    coupled_send,
+    coupled_recv,
+    inner_send,
+    inner_recv,
     ket_send,
     ket_recv,
     dipole_send,
@@ -125,17 +149,6 @@
         )
     for other in (after, before):
         pl.semaphore_signal(barrier, inc=1, device_id=(other, me), device_id_type=MESH)
-    pl.semaphore_wait(barrier, n + 1)
-
-    slots_copy = pltpu.make_async_remote_copy(
-        src_ref=right_ref,
-        dst_ref=slots_vmem,
-        send_sem=slot_sem.at[0],
-        recv_sem=slot_sem.at[1],
-        device_id=(after, me),
-        device_id_type=MESH,
-    )
-    slots_copy.start()
 
     ranges = coupled_ranges(0, panels)
 
@@ -162,90 +175,91 @@
         for i in range(ca):
             for j in range(cb):
                 where[(a + i, b + j)] = place
-                partial[place : place + width, :] = total[
+                coupled_part[place : place + width, :] = total[
                     i * width : (i + 1) * width, j * width : (j + 1) * width
                 ]
                 place = place + width
-    coupled_rows = place
-    total_rows = coupled_rows + panels * eig
-    job_rows = max(JOB_ROWS, 8 * n)
-    job_count = total_rows // job_rows
-    coupled_jobs = coupled_rows // job_rows
-    jobs_of_half = (job_count - coupled_jobs) // halves
-
-    copies = {}
-    levels = n.bit_length() - 1
-
-    def digit(job, level):
-        return lax.rem(me // exchanges(n, job)[level], 2)
-
-    def span_after(job, level, flip=False):
-        offset = job * job_rows
-        for below in range(level):
-            place = digit(job, below)
-            if flip and below == level - 1:
-                place = 1 - place
-            offset = offset + place * (job_rows >> (below + 1))
-        return pl.ds(pl.multiple_of(offset, 8), job_rows >> level)
-
-    def landing(job, level):
-        piece = job_rows >> (level + 1)
-        slot = (job + 1) * job_rows - 2 * piece
-        return slice(slot, slot + piece)
-
-    def start(job, phase):
-        level = phase if phase < levels else 2 * levels - 1 - phase
-        if phase < levels:
-            source = partial.at[span_after(job, level + 1, True)]
-            target = landed.at[landing(job, level)]
-        else:
-            source = full.at[span_after(job, level + 1)]
-            target = source
-        partner = me + (1 - 2 * digit(job, level)) * exchanges(n, job)[level]
+
+    def piece(part, owner, rows):
+        return part[pl.ds(pl.multiple_of(owner * rows, 8), rows), :]
+
+    def send(source, target, sends, recvs, d, peer):
         copy = pltpu.make_async_remote_copy(
             src_ref=source,
             dst_ref=target,
-            send_sem=reduce_send.at[job, phase],
-            recv_sem=reduce_recv.at[job, phase],
-            device_id=(sym, partner),
+            send_sem=sends.at[d - 1],
+            recv_sem=recvs.at[d - 1],
+            device_id=(sym, peer),
             device_id_type=MESH,
         )
         copy.start()
-        copies[(job, phase)] = copy
-
-    def finish(job, phase):
-        copies[(job, phase)].wait()
-        if phase < levels:
-            span = span_after(job, phase + 1)
-            target = full if phase == levels - 1 else partial
-            target[span, :] = partial[span, :] + landed[landing(job, phase), :]
-        if phase + 1 < 2 * levels:
-            start(job, phase + 1)
-
-    for job in range(coupled_jobs):
-        start(job, 0)
+        return copy
+
+    def scatter(part, outgoing, landing, sends, recvs, rows):
+        copies = []
+        for d in range(1, n):
+            peer = lax.rem(me + d, n)
+            encode(piece(part, peer, rows), outgoing.at[d - 1])
+            copies.append(send(outgoing.at[d - 1], landing.at[d - 1], sends, recvs, d, peer))
+        return copies
+
+    def gather(copies, part, landing, gathered, sends, recvs, rows):
+        total = piece(part, me, rows)
+        for d in range(1, n):
+            copies[d - 1].wait()
+            total = total + decode(landing.at[d - 1], rows)
+        encode(total, gathered.at[me])
+        return [
+            send(gathered.at[me], gathered.at[me], sends, recvs, d, lax.rem(me + d, n))
+            for d in range(1, n)
+        ]
+
+    pl.semaphore_wait(barrier, n + 1)
+    coupled_rows = place // n
+    coupled_copies = scatter(
+        coupled_part, coupled_out, coupled_in, coupled_send.at[0], coupled_recv.at[0], coupled_rows
+    )
+    slots_copy = pltpu.make_async_remote_copy(
+        src_ref=right_ref,
+        dst_ref=slots_vmem,
+        send_sem=slot_sem.at[0],
+        recv_sem=slot_sem.at[1],
+        device_id=(after, me),
+        device_id_type=MESH,
+    )
+    slots_copy.start()
 
     def project(r, total):
         load(x_hbm, x_buf, x_sem, r).wait()
         return total + contract(split(x_buf[r]), (v_high[r], v_low[r]), ROWS)
 
-    projected = jnp.zeros((eig, panels * width), F32)
-    parts = len(EARLY) + 1
-    for part in range(parts):
-        projected = lax.fori_loop(
-            part * blocks // parts, (part + 1) * blocks // parts, project, projected
-        )
-        if part < parts - 1:
-            for job, phase in EARLY[part]:
-                finish(job, phase)
+    projected = lax.fori_loop(0, blocks, project, jnp.zeros((eig, panels * width), F32))
+    inner_rows = panels * LANES // n
+    inner_copies = []
     for h in range(halves):
         for k in range(panels):
-            at = coupled_rows + (h * panels + k) * LANES
-            partial[at : at + LANES, :] = projected[
+            inner_part[h, k * LANES : (k + 1) * LANES, :] = projected[
                 h * LANES : (h + 1) * LANES, k * width : (k + 1) * width
             ]
-    for job in range(coupled_jobs, job_count):
-        start(job, 0)
+        inner_copies.append(
+            scatter(
+                inner_part.at[h],
+                inner_out.at[h],
+                inner_in.at[h],
+                inner_send.at[0, h],
+                inner_recv.at[0, h],
+                inner_rows,
+            )
+        )
+    coupled_copies = gather(
+        coupled_copies,
+        coupled_part,
+        coupled_in,
+        coupled_all,
+        coupled_send.at[1],
+        coupled_recv.at[1],
+        coupled_rows,
+    )
 
     slots_copy.wait()
     to_smem = pltpu.make_async_copy(slots_vmem, slots_smem, slot_sem.at[2])
@@ -261,16 +275,16 @@
             if k < panels - 1:
                 later = slice((k + 1) * width, panels * width)
                 row = jnp.concatenate(
-                    [full[where[(k, j)] : where[(k, j)] + width, :] for j in range(k + 1, panels)],
+                    [coupled[where[(k, j)] : where[(k, j)] + width, :] for j in range(k + 1, panels)],
                     axis=1,
                 )
                 inner = contract(split(row), split(t_ref[later, later]), PLAIN)
                 t_ref[here, later] = -contract(split(f_ref[k]), split(inner), PLAIN)
 
     def update(h):
-        begin = coupled_rows + h * panels * LANES
+        whole = jnp.concatenate([decode(inner_all.at[h, j], inner_rows) for j in range(n)], axis=0)
         gathered = jnp.concatenate(
-            [full[begin + k * LANES : begin + (k + 1) * LANES, :] for k in range(panels)], axis=1
+            [whole[k * LANES : (k + 1) * LANES, :] for k in range(panels)], axis=1
         )
         high, low = split(contract(split(t_ref[...]), split(gathered), COLUMNS))
         u_high[h] = high
@@ -305,23 +319,28 @@
                 finished(left_ref[0, t], h) * occupied
             ).astype(BF16)
 
+    for h in range(halves):
+        inner_copies[h] = gather(
+            inner_copies[h],
+            inner_part.at[h],
+            inner_in.at[h],
+            inner_all.at[h],
+            inner_send.at[1, h],
+            inner_recv.at[1, h],
+            inner_rows,
+        )
+    for copy in coupled_copies:
+        copy.wait()
+    for j in range(n):
+        coupled[j * coupled_rows : (j + 1) * coupled_rows, :] = decode(coupled_all.at[j], coupled_rows)
+    transfer_matrix()
     to_smem.wait()
-    events = [(job + SKEW * phase, job, phase) for job in range(job_count) for phase in range(2 * levels)]
-    early = [event for part in EARLY for event in part]
-    for _, job, phase in sorted(events):
-        if (job, phase) not in early:
-            finish(job, phase)
-        if phase == 2 * levels - 1:
-            if job == coupled_jobs - 1:
-                transfer_matrix()
-            done = job + 1 - coupled_jobs
-            if done > 0 and done % jobs_of_half == 0:
-                h = done // jobs_of_half - 1
-                update(h)
-                right_blocks(h)
-                if h < halves - 1:
-                    left_blocks(h)
-    left_blocks(halves - 1)
+    for h in range(halves):
+        for copy in inner_copies[h]:
+            copy.wait()
+        update(h)
+        right_blocks(h)
+        left_blocks(h)
 
     share = eig // n
     tiles_copy.wait()
@@ -374,11 +393,10 @@
     count, width, _ = factors.shape[1:]
     tile_slots = tiles.shape[1]
     halves = eig // LANES
-    phases = 2 * (n.bit_length() - 1)
     blocks = rows // BLOCK
-    coupled_rows = count * (count - 1) // 2 * width
-    reduced = coupled_rows + count * eig
-    jobs = reduced // max(JOB_ROWS, 8 * n)
+    coupled = count * (count - 1) // 2 * width
+    coupled_piece = padded(coupled // n) + PACK
+    inner_piece = padded(count * LANES // n) + PACK
     share = eig // n
     dma = pltpu.SemaphoreType.DMA
     vmem = pl.BlockSpec(memory_space=pltpu.VMEM)
@@ -396,9 +414,15 @@
             pltpu.VMEM((blocks, BLOCK, count * width), BF16),
             pltpu.VMEM((1, tile_slots), jnp.int32),
             pltpu.SMEM((1, tile_slots), jnp.int32),
-            pltpu.VMEM((reduced, width), F32),
-            pltpu.VMEM((reduced, width), F32),
-            pltpu.VMEM((reduced, width), F32),
+            pltpu.VMEM((coupled, LANES), F32),
+            pltpu.VMEM((n - 1, coupled_piece, LANES), I16),
+            pltpu.VMEM((n - 1, coupled_piece, LANES), I16),
+            pltpu.VMEM((n, coupled_piece, LANES), I16),
+            pltpu.VMEM((coupled, LANES), F32),
+            pltpu.VMEM((halves, count * LANES, LANES), F32),
+            pltpu.VMEM((halves, n - 1, inner_piece, LANES), I16),
+            pltpu.VMEM((halves, n - 1, inner_piece, LANES), I16),
+            pltpu.VMEM((halves, n, inner_piece, LANES), I16),
             pltpu.VMEM((count * width, count * width), F32),
             pltpu.VMEM((halves, count * width, LANES), BF16),
             pltpu.VMEM((halves, count * width, LANES), BF16),
@@ -414,8 +438,10 @@
             dma((blocks,)),
             dma((3,)),
             dma((2,)),
-            dma((jobs, phases)),
-            dma((jobs, phases)),
+            dma((2, n - 1)),
+            dma((2, n - 1)),
+            dma((2, halves, n - 1)),
+            dma((2, halves, n - 1)),
             dma((halves, tile_slots)),
             dma((halves, tile_slots)),
             dma((halves, n - 1)),

time: 58.3 us -> 53.8 us (0.923)
  Pallas kernels: 56.8 us -> 52.3 us
    pallas_call x1, Pallas kernels: 56.8 us -> 52.3 us  [on_device(): pl.pallas_call(functools.partial(kernel, n, syms), out_shape=jax.ShapeDty...]
where the time goes in v1:
time: 53.8 us; the launch traced here: 53.6 us
  Pallas kernels  52.3 us (97%)
  local copies, waits for them, and re-layouts  1.38 us (3%)
    pallas_call x1, Pallas kernels, on_device(): pl.pallas_call(functools.partial(kernel, n, syms), out_shape=jax.ShapeDty...  52.3 us
    unnamed x1, local copies, waits for them, and re-layouts  1.38 us

profile of v1, /device:TPU:1, one launch (start us, length us, event | category | flops | bytes accessed | tf_op | source)
XLA Modules:
  0.0 53.6 jit_solution(1603514827966644672)
XLA Ops:
  0.0 52.3 %shard_map.82 = f32[1,32,256]{2,1,0:T(8,128)} custom-call(f32[8,512,256]{2,1,0:T(8,128)} %bitcast.5, f32[8,512,512]{2,1,0:T(8,128)} %bitcast.4, f32[4,128,128]{2,1,0:T(8,128)} %bitcast.7, bf16[2,512,512]{2,1,0:T(8,128)(2,1)} %bitcast.6, s32[1,2]{1,0:T(1,128)} %right_ref.1, s32[1,2]{1,0:T(1,128)} %left_ref.1, s32[1,2]{1,0:T(1,128)} %occupied_ref.1, ...), custom_call_target="tpu_custom_call" | custom-call | tf_op jit(solution)/shard_map/pallas_call | solution.py:405
  52.3 1.4 %copy.10 = f32[1,32,256]{2,1,0:T(8,128)} copy(f32[1,32,256]{2,1,0:T(8,128)} %shard_map.82) | data formatting | bytes 65536

commit v2 on v1

--- a/solution.py
+++ b/solution.py
@@ -9,6 +9,8 @@
 
 BLOCK = 512
 LANES = 128
+COUPLE_SPAN = 2
+PROJECT_SPAN = 4
 PACK = 16
 TOP = 15.0
 MARGIN = 1e-3
@@ -40,12 +42,15 @@
 COLUMNS = ((1,), (1,))
 
 
-def coupled_ranges(first, count):
-    if count < 2:
-        return []
-    half = count // 2
-    here = [(first, half, first + half, count - half)]
-    return here + coupled_ranges(first, half) + coupled_ranges(first + half, count - half)
+def couplings(panels):
+    levels = []
+    size = panels
+    while size > 1:
+        starts = range(0, panels, size)
+        first = [a + i for a in starts for i in range(size // 2)]
+        levels.append((first, [a + size // 2 for a in first], size // 2))
+        size //= 2
+    return levels
 
 
 def padded(rows):
@@ -96,6 +101,8 @@
     inner_out,
     inner_in,
     inner_all,
+    inner,
+    x_turned,
     t_ref,
     u_high,
     u_low,
@@ -150,35 +157,46 @@
     for other in (after, before):
         pl.semaphore_signal(barrier, inc=1, device_id=(other, me), device_id_type=MESH)
 
-    ranges = coupled_ranges(0, panels)
+    levels = couplings(panels)
+
+    def side(both, chosen):
+        return tuple(
+            jnp.concatenate([half[:, k * width : (k + 1) * width] for k in chosen], axis=1)
+            for half in both
+        )
 
     def couple(r, sums):
-        load(v_hbm, v_buf, v_sem, r).wait()
-        high, low = split(v_buf[r])
-        v_high[r] = high
-        v_low[r] = low
-        out = []
-        for total, (a, ca, b, cb) in zip(sums, ranges):
-            pa = slice(a * width, (a + ca) * width)
-            pb = slice(b * width, (b + cb) * width)
-            out.append(
-                total + contract((high[:, pa], low[:, pa]), (high[:, pb], low[:, pb]), ROWS)
-            )
-        return tuple(out)
-
+        parts = []
+        for i in range(COUPLE_SPAN):
+            block = r * COUPLE_SPAN + i
+            load(v_hbm, v_buf, v_sem, block).wait()
+            both = split(v_buf[block])
+            v_high[block], v_low[block] = both
+            parts.append(both)
+        both = tuple(jnp.concatenate(half, axis=0) for half in zip(*parts))
+        return tuple(
+            total + contract(side(both, first), side(both, second), ROWS)
+            for total, (first, second, _) in zip(sums, levels)
+        )
+
+    half_width = panels // 2 * width
     sums = lax.fori_loop(
-        0, blocks, couple, tuple(jnp.zeros((ca * width, cb * width), F32) for _, ca, _, cb in ranges)
+        0,
+        blocks // COUPLE_SPAN,
+        couple,
+        tuple(jnp.zeros((half_width, half_width), F32) for _ in levels),
     )
     where = {}
     place = 0
-    for total, (a, ca, b, cb) in zip(sums, ranges):
-        for i in range(ca):
-            for j in range(cb):
-                where[(a + i, b + j)] = place
-                coupled_part[place : place + width, :] = total[
-                    i * width : (i + 1) * width, j * width : (j + 1) * width
-                ]
-                place = place + width
+    for total, (first, second, size) in zip(sums, levels):
+        for i, a in enumerate(first):
+            for j, b in enumerate(second):
+                if i // size == j // size:
+                    where[(a, b)] = place
+                    coupled_part[place : place + width, :] = total[
+                        i * width : (i + 1) * width, j * width : (j + 1) * width
+                    ]
+                    place = place + width
 
     def piece(part, owner, rows):
         return part[pl.ds(pl.multiple_of(owner * rows, 8), rows), :]
@@ -203,11 +221,14 @@
             copies.append(send(outgoing.at[d - 1], landing.at[d - 1], sends, recvs, d, peer))
         return copies
 
-    def gather(copies, part, landing, gathered, sends, recvs, rows):
+    def collect(copies, part, landing, rows):
         total = piece(part, me, rows)
         for d in range(1, n):
             copies[d - 1].wait()
             total = total + decode(landing.at[d - 1], rows)
+        return total
+
+    def gather(total, gathered, sends, recvs):
         encode(total, gathered.at[me])
         return [
             send(gathered.at[me], gathered.at[me], sends, recvs, d, lax.rem(me + d, n))
@@ -229,36 +250,55 @@
     )
     slots_copy.start()
 
-    def project(r, total):
-        load(x_hbm, x_buf, x_sem, r).wait()
-        return total + contract(split(x_buf[r]), (v_high[r], v_low[r]), ROWS)
-
-    projected = lax.fori_loop(0, blocks, project, jnp.zeros((eig, panels * width), F32))
-    inner_rows = panels * LANES // n
+    share = LANES // n
+    pairs = panels // 2
+    inner_rows = halves * 2 * share
     inner_copies = []
-    for h in range(halves):
-        for k in range(panels):
-            inner_part[h, k * LANES : (k + 1) * LANES, :] = projected[
-                h * LANES : (h + 1) * LANES, k * width : (k + 1) * width
-            ]
+    for q in range(pairs):
+        columns = slice(2 * q * width, 2 * (q + 1) * width)
+
+        def project(r, total):
+            span = pl.ds(r * PROJECT_SPAN, PROJECT_SPAN)
+            rows = PROJECT_SPAN * BLOCK
+            if q == 0:
+                for i in range(PROJECT_SPAN):
+                    load(x_hbm, x_buf, x_sem, r * PROJECT_SPAN + i).wait()
+                high, low = split(x_buf[span].reshape(rows, eig))
+                x_turned[0, r] = high.T
+                x_turned[1, r] = low.T
+            high, low = x_turned[0, r], x_turned[1, r]
+            both = (
+                v_high[span, :, columns].reshape(rows, 2 * width),
+                v_low[span, :, columns].reshape(rows, 2 * width),
+            )
+            return total + contract((high, low), both, PLAIN)
+
+        projected = lax.fori_loop(
+            0, blocks // PROJECT_SPAN, project, jnp.zeros((eig, 2 * width), F32)
+        )
+        for d in range(n):
+            for h in range(halves):
+                for k in range(2):
+                    source = h * LANES + d * share
+                    target = (d * halves + h) * 2 * share + k * share
+                    inner_part[q, target : target + share, :] = projected[
+                        source : source + share, k * width : (k + 1) * width
+                    ]
         inner_copies.append(
             scatter(
-                inner_part.at[h],
-                inner_out.at[h],
-                inner_in.at[h],
-                inner_send.at[0, h],
-                inner_recv.at[0, h],
+                inner_part.at[q],
+                inner_out.at[q],
+                inner_in.at[q],
+                inner_send.at[0, q],
+                inner_recv.at[0, q],
                 inner_rows,
             )
         )
     coupled_copies = gather(
-        coupled_copies,
-        coupled_part,
-        coupled_in,
+        collect(coupled_copies, coupled_part, coupled_in, coupled_rows),
         coupled_all,
         coupled_send.at[1],
         coupled_recv.at[1],
-        coupled_rows,
     )
 
     slots_copy.wait()
@@ -282,25 +322,29 @@
                 t_ref[here, later] = -contract(split(f_ref[k]), split(inner), PLAIN)
 
     def update(h):
-        whole = jnp.concatenate([decode(inner_all.at[h, j], inner_rows) for j in range(n)], axis=0)
-        gathered = jnp.concatenate(
-            [whole[k * LANES : (k + 1) * LANES, :] for k in range(panels)], axis=1
-        )
-        high, low = split(contract(split(t_ref[...]), split(gathered), COLUMNS))
-        u_high[h] = high
-        u_low[h] = low
-
-    def finished(slot, h):
-        change = contract((v_high[slot], v_low[slot]), (u_high[h], u_low[h]), PLAIN)
-        live = lax.broadcasted_iota(jnp.int32, (BLOCK, LANES), 0) < channels_ref[0, slot]
-        value = x_buf[slot, :, h * LANES : (h + 1) * LANES] - change
+        for j in range(n):
+            value = decode(inner_all.at[h, j], panels * share)
+            for k in range(panels):
+                inner[h, j * share : (j + 1) * share, k * width : (k + 1) * width] = value[
+                    k * share : (k + 1) * share, :
+                ]
+        high, low = split(contract(split(t_ref[...]), split(inner[h]), COLUMNS))
+        u_high[:, h * LANES : (h + 1) * LANES] = high
+        u_low[:, h * LANES : (h + 1) * LANES] = low
+
+    def finished(slot, columns):
+        change = contract(
+            (v_high[slot], v_low[slot]), (u_high[:, columns], u_low[:, columns]), PLAIN
+        )
+        value = x_buf[slot, :, columns] - change
+        live = lax.broadcasted_iota(jnp.int32, value.shape, 0) < channels_ref[0, slot]
         return jnp.where(live, value, 0.0)
 
     kets = {}
 
     def right_blocks(h):
         for t in range(tile_slots):
-            ket_out[h, t] = finished(slots_smem[0, t], h).astype(BF16)
+            ket_out[h, t] = finished(slots_smem[0, t], slice(h * LANES, (h + 1) * LANES)).astype(BF16)
             copy = pltpu.make_async_remote_copy(
                 src_ref=ket_out.at[h, t],
                 dst_ref=ket_in.at[h, t],
@@ -312,23 +356,25 @@
             copy.start()
             kets[(h, t)] = copy
 
-    def left_blocks(h):
+    def left_blocks():
         for t in range(tile_slots):
             occupied = occupied_ref[0, t].astype(F32)
-            bras[t, :, h * LANES : (h + 1) * LANES] = (
-                finished(left_ref[0, t], h) * occupied
-            ).astype(BF16)
-
-    for h in range(halves):
-        inner_copies[h] = gather(
-            inner_copies[h],
-            inner_part.at[h],
-            inner_in.at[h],
+            bras[t] = (finished(left_ref[0, t], slice(0, eig)) * occupied).astype(BF16)
+
+    totals = [
+        collect(inner_copies[q], inner_part.at[q], inner_in.at[q], inner_rows) for q in range(pairs)
+    ]
+    inner_copies = [
+        gather(
+            jnp.concatenate(
+                [total[h * 2 * share : (h + 1) * 2 * share, :] for total in totals], axis=0
+            ),
             inner_all.at[h],
             inner_send.at[1, h],
             inner_recv.at[1, h],
-            inner_rows,
-        )
+        )
+        for h in range(halves)
+    ]
     for copy in coupled_copies:
         copy.wait()
     for j in range(n):
@@ -340,9 +386,9 @@
             copy.wait()
         update(h)
         right_blocks(h)
-        left_blocks(h)
-
-    share = eig // n
+    left_blocks()
+
+    own_rows = eig // n
     tiles_copy.wait()
     sends = []
     for h in range(halves):
@@ -353,8 +399,8 @@
             total = total + lax.dot_general(
                 bras[t], product, (ROWS, ((), ())), preferred_element_type=F32
             )
-        own[h] = total.reshape(n, share, LANES)
-        dipole_out[h] = total.reshape(n, share, LANES).astype(BF16)
+        own[h] = total.reshape(n, own_rows, LANES)
+        dipole_out[h] = total.reshape(n, own_rows, LANES).astype(BF16)
         for d in range(1, n):
             target = lax.rem(me + d, n)
             copy = pltpu.make_async_remote_copy(
@@ -396,7 +442,9 @@
     blocks = rows // BLOCK
     coupled = count * (count - 1) // 2 * width
     coupled_piece = padded(coupled // n) + PACK
+    scatter_piece = padded(2 * eig // n) + PACK
     inner_piece = padded(count * LANES // n) + PACK
+    spans = blocks // PROJECT_SPAN
     share = eig // n
     dma = pltpu.SemaphoreType.DMA
     vmem = pl.BlockSpec(memory_space=pltpu.VMEM)
@@ -419,13 +467,15 @@
             pltpu.VMEM((n - 1, coupled_piece, LANES), I16),
             pltpu.VMEM((n, coupled_piece, LANES), I16),
             pltpu.VMEM((coupled, LANES), F32),
-            pltpu.VMEM((halves, count * LANES, LANES), F32),
-            pltpu.VMEM((halves, n - 1, inner_piece, LANES), I16),
-            pltpu.VMEM((halves, n - 1, inner_piece, LANES), I16),
+            pltpu.VMEM((count // 2, 2 * eig, LANES), F32),
+            pltpu.VMEM((count // 2, n - 1, scatter_piece, LANES), I16),
+            pltpu.VMEM((count // 2, n - 1, scatter_piece, LANES), I16),
             pltpu.VMEM((halves, n, inner_piece, LANES), I16),
+            pltpu.VMEM((halves, LANES, count * width), F32),
+            pltpu.VMEM((2, spans, eig, rows // spans), BF16),
             pltpu.VMEM((count * width, count * width), F32),
-            pltpu.VMEM((halves, count * width, LANES), BF16),
-            pltpu.VMEM((halves, count * width, LANES), BF16),
+            pltpu.VMEM((count * width, eig), BF16),
+            pltpu.VMEM((count * width, eig), BF16),
             pltpu.VMEM((halves, tile_slots, BLOCK, LANES), BF16),
             pltpu.VMEM((halves, tile_slots, BLOCK, LANES), BF16),
             pltpu.VMEM((tile_slots, BLOCK, eig), BF16),
@@ -440,8 +490,8 @@
             dma((2,)),
             dma((2, n - 1)),
             dma((2, n - 1)),
-            dma((2, halves, n - 1)),
-            dma((2, halves, n - 1)),
+            dma((2, max(halves, count // 2), n - 1)),
+            dma((2, max(halves, count // 2), n - 1)),
             dma((halves, tile_slots)),
             dma((halves, tile_slots)),
             dma((halves, n - 1)),

time: 53.8 us -> 52.1 us (0.968)
  Pallas kernels: 52.3 us -> 50.6 us
    pallas_call x1, Pallas kernels: 52.3 us -> 50.6 us  [on_device(): pl.pallas_call(functools.partial(kernel, n, syms), out_shape=jax.ShapeDty...]
where the time goes in v2:
time: 52.1 us; the launch traced here: 51.9 us
  Pallas kernels  50.6 us (97%)
  local copies, waits for them, and re-layouts  1.38 us (3%)
    pallas_call x1, Pallas kernels, on_device(): pl.pallas_call(functools.partial(kernel, n, syms), out_shape=jax.ShapeDty...  50.6 us
    unnamed x1, local copies, waits for them, and re-layouts  1.38 us

profile of v2, /device:TPU:1, one launch (start us, length us, event | category | flops | bytes accessed | tf_op | source)
XLA Modules:
  0.0 51.9 jit_solution(8404895331289586886)
XLA Ops:
  0.0 50.6 %shard_map.82 = f32[1,32,256]{2,1,0:T(8,128)} custom-call(f32[8,512,256]{2,1,0:T(8,128)} %bitcast.5, f32[8,512,512]{2,1,0:T(8,128)} %bitcast.4, f32[4,128,128]{2,1,0:T(8,128)} %bitcast.7, bf16[2,512,512]{2,1,0:T(8,128)(2,1)} %bitcast.6, s32[1,2]{1,0:T(1,128)} %right_ref.1, s32[1,2]{1,0:T(1,128)} %left_ref.1, s32[1,2]{1,0:T(1,128)} %occupied_ref.1, ...), custom_call_target="tpu_custom_call" | custom-call | tf_op jit(solution)/shard_map/pallas_call | solution.py:453
  50.6 1.4 %copy.10 = f32[1,32,256]{2,1,0:T(8,128)} copy(f32[1,32,256]{2,1,0:T(8,128)} %shard_map.82) | data formatting | bytes 65536

commit v3 on v2

--- a/solution.py
+++ b/solution.py
@@ -27,14 +27,15 @@
     return high, (value - high.astype(F32)).astype(BF16)
 
 
+def multiply(a, b, dims):
+    return lax.dot_general(a, b, (dims, ((), ())), preferred_element_type=F32)
+
+
 def contract(first, second, dims):
     high, low = first
     other_high, other_low = second
-
-    def dot(a, b):
-        return lax.dot_general(a, b, (dims, ((), ())), preferred_element_type=F32)
-
-    return dot(high, other_high) + (dot(high, other_low) + dot(low, other_high))
+    crossed = multiply(high, other_low, dims) + multiply(low, other_high, dims)
+    return multiply(high, other_high, dims) + crossed
 
 
 ROWS = ((0,), (0,))
@@ -159,23 +160,23 @@
 
     levels = couplings(panels)
 
-    def side(both, chosen):
-        return tuple(
-            jnp.concatenate([half[:, k * width : (k + 1) * width] for k in chosen], axis=1)
-            for half in both
-        )
+    def side(ref, span, chosen):
+        rows = ref[span].reshape(COUPLE_SPAN * BLOCK, panels * width)
+        return jnp.concatenate([rows[:, k * width : (k + 1) * width] for k in chosen], axis=1)
 
     def couple(r, sums):
-        parts = []
         for i in range(COUPLE_SPAN):
             block = r * COUPLE_SPAN + i
             load(v_hbm, v_buf, v_sem, block).wait()
-            both = split(v_buf[block])
-            v_high[block], v_low[block] = both
-            parts.append(both)
-        both = tuple(jnp.concatenate(half, axis=0) for half in zip(*parts))
+            v_high[block], v_low[block] = split(v_buf[block])
+        span = pl.ds(r * COUPLE_SPAN, COUPLE_SPAN)
         return tuple(
-            total + contract(side(both, first), side(both, second), ROWS)
+            total
+            + contract(
+                (side(v_high, span, first), side(v_low, span, first)),
+                (side(v_high, span, second), side(v_low, span, second)),
+                ROWS,
+            )
             for total, (first, second, _) in zip(sums, levels)
         )
 
@@ -187,16 +188,20 @@
         tuple(jnp.zeros((half_width, half_width), F32) for _ in levels),
     )
     where = {}
+    blocks_of = [
+        (total, first[i], second[j], i, j, i // size == j // size)
+        for total, (first, second, size) in zip(sums, levels)
+        for i in range(len(first))
+        for j in range(len(second))
+    ]
     place = 0
-    for total, (first, second, size) in zip(sums, levels):
-        for i, a in enumerate(first):
-            for j, b in enumerate(second):
-                if i // size == j // size:
-                    where[(a, b)] = place
-                    coupled_part[place : place + width, :] = total[
-                        i * width : (i + 1) * width, j * width : (j + 1) * width
-                    ]
-                    place = place + width
+    for total, a, b, i, j, needed in sorted(blocks_of, key=lambda entry: not entry[-1]):
+        coupled_part[place : place + width, :] = total[
+            i * width : (i + 1) * width, j * width : (j + 1) * width
+        ]
+        if needed:
+            where[(a, b)] = place
+        place = place + width
 
     def piece(part, owner, rows):
         return part[pl.ds(pl.multiple_of(owner * rows, 8), rows), :]
@@ -236,7 +241,7 @@
         ]
 
     pl.semaphore_wait(barrier, n + 1)
-    coupled_rows = place // n
+    coupled_rows = len(where) * width // n
     coupled_copies = scatter(
         coupled_part, coupled_out, coupled_in, coupled_send.at[0], coupled_recv.at[0], coupled_rows
     )
@@ -260,18 +265,21 @@
         def project(r, total):
             span = pl.ds(r * PROJECT_SPAN, PROJECT_SPAN)
             rows = PROJECT_SPAN * BLOCK
+            both = (
+                v_high[span, :, columns].reshape(rows, 2 * width),
+                v_low[span, :, columns].reshape(rows, 2 * width),
+            )
             if q == 0:
                 for i in range(PROJECT_SPAN):
                     load(x_hbm, x_buf, x_sem, r * PROJECT_SPAN + i).wait()
                 high, low = split(x_buf[span].reshape(rows, eig))
-                x_turned[0, r] = high.T
-                x_turned[1, r] = low.T
-            high, low = x_turned[0, r], x_turned[1, r]
-            both = (
-                v_high[span, :, columns].reshape(rows, 2 * width),
-                v_low[span, :, columns].reshape(rows, 2 * width),
-            )
-            return total + contract((high, low), both, PLAIN)
+                x_turned[r, :eig, :] = high.T
+                x_turned[r, eig:, :] = low.T
+                turned = (x_turned[r, :eig, :], x_turned[r, eig:, :])
+                return total + contract(turned, both, PLAIN)
+            fine = multiply(x_turned[r], both[0], PLAIN)
+            crossed = multiply(x_turned[r, :eig, :], both[1], PLAIN)
+            return total + (fine[:eig] + (fine[eig:] + crossed))
 
         projected = lax.fori_loop(
             0, blocks // PROJECT_SPAN, project, jnp.zeros((eig, 2 * width), F32)
@@ -442,6 +450,7 @@
     blocks = rows // BLOCK
     coupled = count * (count - 1) // 2 * width
     coupled_piece = padded(coupled // n) + PACK
+    products = len(couplings(count)) * (count // 2) ** 2 * width
     scatter_piece = padded(2 * eig // n) + PACK
     inner_piece = padded(count * LANES // n) + PACK
     spans = blocks // PROJECT_SPAN
@@ -462,7 +471,7 @@
             pltpu.VMEM((blocks, BLOCK, count * width), BF16),
             pltpu.VMEM((1, tile_slots), jnp.int32),
             pltpu.SMEM((1, tile_slots), jnp.int32),
-            pltpu.VMEM((coupled, LANES), F32),
+            pltpu.VMEM((products, LANES), F32),
             pltpu.VMEM((n - 1, coupled_piece, LANES), I16),
             pltpu.VMEM((n - 1, coupled_piece, LANES), I16),
             pltpu.VMEM((n, coupled_piece, LANES), I16),
@@ -472,7 +481,7 @@
             pltpu.VMEM((count // 2, n - 1, scatter_piece, LANES), I16),
             pltpu.VMEM((halves, n, inner_piece, LANES), I16),
             pltpu.VMEM((halves, LANES, count * width), F32),
-            pltpu.VMEM((2, spans, eig, rows // spans), BF16),
+            pltpu.VMEM((spans, 2 * eig, rows // spans), BF16),
             pltpu.VMEM((count * width, count * width), F32),
             pltpu.VMEM((count * width, eig), BF16),
             pltpu.VMEM((count * width, eig), BF16),

time: 52.1 us -> 52 us (level)
  no operation moved by 1% of the time
where the time goes in v3:
time: 52 us; the launch traced here: 51.8 us
  Pallas kernels  50.4 us (97%)
  local copies, waits for them, and re-layouts  1.38 us (3%)
    pallas_call x1, Pallas kernels, on_device(): pl.pallas_call(functools.partial(kernel, n, syms), out_shape=jax.ShapeDty...  50.4 us
    unnamed x1, local copies, waits for them, and re-layouts  1.38 us

profile of v3, /device:TPU:1, one launch (start us, length us, event | category | flops | bytes accessed | tf_op | source)
XLA Modules:
  0.0 51.8 jit_solution(8400778253180981034)
XLA Ops:
  0.0 50.4 %shard_map.82 = f32[1,32,256]{2,1,0:T(8,128)} custom-call(f32[8,512,256]{2,1,0:T(8,128)} %bitcast.5, f32[8,512,512]{2,1,0:T(8,128)} %bitcast.4, f32[4,128,128]{2,1,0:T(8,128)} %bitcast.7, bf16[2,512,512]{2,1,0:T(8,128)(2,1)} %bitcast.6, s32[1,2]{1,0:T(1,128)} %right_ref.1, s32[1,2]{1,0:T(1,128)} %left_ref.1, s32[1,2]{1,0:T(1,128)} %occupied_ref.1, ...), custom_call_target="tpu_custom_call" | custom-call | tf_op jit(solution)/shard_map/pallas_call | solution.py:462
  50.5 1.4 %copy.10 = f32[1,32,256]{2,1,0:T(8,128)} copy(f32[1,32,256]{2,1,0:T(8,128)} %shard_map.82) | data formatting | bytes 65536

commit v4 on v3

--- a/solution.py
+++ b/solution.py
@@ -11,6 +11,8 @@
 LANES = 128
 COUPLE_SPAN = 2
 PROJECT_SPAN = 4
+RING = 4
+PAIR = 2
 PACK = 16
 TOP = 15.0
 MARGIN = 1e-3
@@ -96,11 +98,13 @@
     coupled_part,
     coupled_out,
     coupled_in,
+    coupled_pass,
     coupled_all,
     coupled,
     inner_part,
     inner_out,
     inner_in,
+    inner_pass,
     inner_all,
     inner,
     x_turned,
@@ -206,44 +210,82 @@
     def piece(part, owner, rows):
         return part[pl.ds(pl.multiple_of(owner * rows, 8), rows), :]
 
-    def send(source, target, sends, recvs, d, peer):
+    def send(source, target, sems, k, peer):
         copy = pltpu.make_async_remote_copy(
             src_ref=source,
             dst_ref=target,
-            send_sem=sends.at[d - 1],
-            recv_sem=recvs.at[d - 1],
+            send_sem=sems[0].at[k],
+            recv_sem=sems[1].at[k],
             device_id=(sym, peer),
             device_id_type=MESH,
         )
         copy.start()
         return copy
 
-    def scatter(part, outgoing, landing, sends, recvs, rows):
-        copies = []
-        for d in range(1, n):
-            peer = lax.rem(me + d, n)
-            encode(piece(part, peer, rows), outgoing.at[d - 1])
-            copies.append(send(outgoing.at[d - 1], landing.at[d - 1], sends, recvs, d, peer))
+    relayed = n == RING * PAIR
+    if relayed:
+        steps = [(a, b) for a in (2, 1, 3, 0) for b in (0, 1) if a or b]
+        peers = [
+            lax.rem(me // PAIR + a, RING) * PAIR + lax.rem(me + b, PAIR) for a, b in steps
+        ]
+    else:
+        steps = []
+        peers = [lax.rem(me + d, n) for d in range(1, n)]
+
+    def scatter(part, outgoing, landing, passing, sems, rows):
+        copies = {}
+        order = sorted(range(n - 1), key=lambda k: relayed and steps[k] != (2, 1))
+        for k in order:
+            encode(piece(part, peers[k], rows), outgoing.at[k])
+            if relayed and steps[k] == (2, 1):
+                near = peers[steps.index((3, 1))]
+                copies["first"] = send(outgoing.at[k], passing, sems, n - 1, near)
+            else:
+                copies[k] = send(outgoing.at[k], landing.at[k], sems, k, peers[k])
         return copies
+
+    def pass_on(copies, landing, passing, sems):
+        if relayed:
+            copies.pop("first").wait()
+            k = steps.index((2, 1))
+            copies[k] = send(passing, landing.at[k], sems, k, peers[steps.index((3, 0))])
 
     def collect(copies, part, landing, rows):
         total = piece(part, me, rows)
-        for d in range(1, n):
-            copies[d - 1].wait()
-            total = total + decode(landing.at[d - 1], rows)
+        for k in copies:
+            copies[k].wait()
+            total = total + decode(landing.at[k], rows)
         return total
 
-    def gather(total, gathered, sends, recvs):
+    def gather(total, gathered, sems):
         encode(total, gathered.at[me])
-        return [
-            send(gathered.at[me], gathered.at[me], sends, recvs, d, lax.rem(me + d, n))
-            for d in range(1, n)
-        ]
+        return {
+            k: send(gathered.at[me], gathered.at[me], sems, k, peers[k])
+            for k in range(n - 1)
+            if not (relayed and steps[k][0] == 2)
+        }
+
+    def hand_on(copies, gathered, sems):
+        if relayed:
+            for b, ahead in ((0, 1), (1, 3)):
+                copies[steps.index((ahead, b))].wait_recv()
+                behind = lax.rem(me // PAIR + RING - ahead, RING) * PAIR + lax.rem(me + b, PAIR)
+                k = steps.index((2, b))
+                peer = peers[steps.index((ahead, 0))]
+                copies[k] = send(gathered.at[behind], gathered.at[behind], sems, k, peer)
+
+    def finish(copies):
+        for k in copies:
+            if relayed and steps[k] in ((1, 0), (3, 1)):
+                copies[k].wait_send()
+            else:
+                copies[k].wait()
 
     pl.semaphore_wait(barrier, n + 1)
     coupled_rows = len(where) * width // n
+    coupled_sems = [(coupled_send.at[i], coupled_recv.at[i]) for i in range(2)]
     coupled_copies = scatter(
-        coupled_part, coupled_out, coupled_in, coupled_send.at[0], coupled_recv.at[0], coupled_rows
+        coupled_part, coupled_out, coupled_in, coupled_pass, coupled_sems[0], coupled_rows
     )
     slots_copy = pltpu.make_async_remote_copy(
         src_ref=right_ref,
@@ -258,6 +300,10 @@
     share = LANES // n
     pairs = panels // 2
     inner_rows = halves * 2 * share
+    inner_sems = [
+        [(inner_send.at[i, h], inner_recv.at[i, h]) for h in range(max(pairs, halves))]
+        for i in range(2)
+    ]
     inner_copies = []
     for q in range(pairs):
         columns = slice(2 * q * width, 2 * (q + 1) * width)
@@ -297,17 +343,19 @@
                 inner_part.at[q],
                 inner_out.at[q],
                 inner_in.at[q],
-                inner_send.at[0, q],
-                inner_recv.at[0, q],
+                inner_pass.at[q],
+                inner_sems[0][q],
                 inner_rows,
             )
         )
+        if q == 0:
+            pass_on(coupled_copies, coupled_in, coupled_pass, coupled_sems[0])
+        else:
+            pass_on(inner_copies[q - 1], inner_in.at[q - 1], inner_pass.at[q - 1], inner_sems[0][q - 1])
     coupled_copies = gather(
-        collect(coupled_copies, coupled_part, coupled_in, coupled_rows),
-        coupled_all,
-        coupled_send.at[1],
-        coupled_recv.at[1],
+        collect(coupled_copies, coupled_part, coupled_in, coupled_rows), coupled_all, coupled_sems[1]
     )
+    pass_on(inner_copies[-1], inner_in.at[pairs - 1], inner_pass.at[pairs - 1], inner_sems[0][pairs - 1])
 
     slots_copy.wait()
     to_smem = pltpu.make_async_copy(slots_vmem, slots_smem, slot_sem.at[2])
@@ -378,20 +426,20 @@
                 [total[h * 2 * share : (h + 1) * 2 * share, :] for total in totals], axis=0
             ),
             inner_all.at[h],
-            inner_send.at[1, h],
-            inner_recv.at[1, h],
+            inner_sems[1][h],
         )
         for h in range(halves)
     ]
-    for copy in coupled_copies:
-        copy.wait()
+    hand_on(coupled_copies, coupled_all, coupled_sems[1])
+    for h in range(halves):
+        hand_on(inner_copies[h], inner_all.at[h], inner_sems[1][h])
+    finish(coupled_copies)
     for j in range(n):
         coupled[j * coupled_rows : (j + 1) * coupled_rows, :] = decode(coupled_all.at[j], coupled_rows)
     transfer_matrix()
     to_smem.wait()
     for h in range(halves):
-        for copy in inner_copies[h]:
-            copy.wait()
+        finish(inner_copies[h])
         update(h)
         right_blocks(h)
     left_blocks()
@@ -474,11 +522,13 @@
             pltpu.VMEM((products, LANES), F32),
             pltpu.VMEM((n - 1, coupled_piece, LANES), I16),
             pltpu.VMEM((n - 1, coupled_piece, LANES), I16),
+            pltpu.VMEM((coupled_piece, LANES), I16),
             pltpu.VMEM((n, coupled_piece, LANES), I16),
             pltpu.VMEM((coupled, LANES), F32),
             pltpu.VMEM((count // 2, 2 * eig, LANES), F32),
             pltpu.VMEM((count // 2, n - 1, scatter_piece, LANES), I16),
             pltpu.VMEM((count // 2, n - 1, scatter_piece, LANES), I16),
+            pltpu.VMEM((count // 2, scatter_piece, LANES), I16),
             pltpu.VMEM((halves, n, inner_piece, LANES), I16),
             pltpu.VMEM((halves, LANES, count * width), F32),
             pltpu.VMEM((spans, 2 * eig, rows // spans), BF16),
@@ -497,10 +547,10 @@
             dma((blocks,)),
             dma((3,)),
             dma((2,)),
-            dma((2, n - 1)),
-            dma((2, n - 1)),
-            dma((2, max(halves, count // 2), n - 1)),
-            dma((2, max(halves, count // 2), n - 1)),
+            dma((2, n)),
+            dma((2, n)),
+            dma((2, max(halves, count // 2), n)),
+            dma((2, max(halves, count // 2), n)),
             dma((halves, tile_slots)),
             dma((halves, tile_slots)),
             dma((halves, n - 1)),

time: 52 us -> 52.9 us (1.017)
  Pallas kernels: 50.4 us -> 51.3 us
    pallas_call x1, Pallas kernels: 50.4 us -> 51.3 us  [on_device(): pl.pallas_call(functools.partial(kernel, n, syms), out_shape=jax.ShapeDty...]
where the time goes in v4:
time: 52.9 us; the launch traced here: 52.7 us
  Pallas kernels  51.3 us (97%)
  local copies, waits for them, and re-layouts  1.38 us (3%)
    pallas_call x1, Pallas kernels, on_device(): pl.pallas_call(functools.partial(kernel, n, syms), out_shape=jax.ShapeDty...  51.3 us
    unnamed x1, local copies, waits for them, and re-layouts  1.38 us

profile of v4, /device:TPU:1, one launch (start us, length us, event | category | flops | bytes accessed | tf_op | source)
XLA Modules:
  0.0 52.7 jit_solution(3306074932738768204)
XLA Ops:
  0.0 51.3 %shard_map.82 = f32[1,32,256]{2,1,0:T(8,128)} custom-call(f32[8,512,256]{2,1,0:T(8,128)} %bitcast.5, f32[8,512,512]{2,1,0:T(8,128)} %bitcast.4, f32[4,128,128]{2,1,0:T(8,128)} %bitcast.7, bf16[2,512,512]{2,1,0:T(8,128)(2,1)} %bitcast.6, s32[1,2]{1,0:T(1,128)} %right_ref.1, s32[1,2]{1,0:T(1,128)} %left_ref.1, s32[1,2]{1,0:T(1,128)} %occupied_ref.1, ...), custom_call_target="tpu_custom_call" | custom-call | tf_op jit(solution)/shard_map/pallas_call | solution.py:510
  51.3 1.4 %copy.10 = f32[1,32,256]{2,1,0:T(8,128)} copy(f32[1,32,256]{2,1,0:T(8,128)} %shard_map.82) | data formatting | bytes 65536

commit v5 on v3

--- a/solution.py
+++ b/solution.py
@@ -11,6 +11,8 @@
 LANES = 128
 COUPLE_SPAN = 2
 PROJECT_SPAN = 4
+RING = 4
+PAIR = 2
 PACK = 16
 TOP = 15.0
 MARGIN = 1e-3
@@ -105,6 +107,8 @@
     inner,
     x_turned,
     t_ref,
+    w_high,
+    w_low,
     u_high,
     u_low,
     ket_out,
@@ -233,12 +237,39 @@
             total = total + decode(landing.at[d - 1], rows)
         return total
 
-    def gather(total, gathered, sends, recvs):
+    ring = n == RING * PAIR
+    steps = [(a, b) for a in (2, 1, 3, 0) for b in (0, 1) if a or b]
+
+    def at(a, b):
+        return lax.rem(me // PAIR + a, RING) * PAIR + lax.rem(me + b, PAIR)
+
+    def gather(total, gathered, sends, recvs, ringed=False):
         encode(total, gathered.at[me])
-        return [
-            send(gathered.at[me], gathered.at[me], sends, recvs, d, lax.rem(me + d, n))
-            for d in range(1, n)
-        ]
+        source = gathered.at[me]
+        if ringed:
+            return {
+                (a, b): send(source, source, sends, recvs, 1 + steps.index((a, b)), at(a, b))
+                for a, b in steps
+                if a != 2
+            }
+        return {
+            d: send(source, source, sends, recvs, d, lax.rem(me + d, n)) for d in range(1, n)
+        }
+
+    def hand_on(copies, gathered, sends, recvs):
+        for a, b in ((1, 0), (3, 1)):
+            copies[(a, b)].wait_recv()
+            source = gathered.at[at(RING - a, b)]
+            copies[(2, b)] = send(
+                source, source, sends, recvs, 1 + steps.index((2, b)), at(a, 0)
+            )
+
+    def finish(copies):
+        for key, copy in copies.items():
+            if key in ((1, 0), (3, 1)):
+                copy.wait_send()
+            else:
+                copy.wait()
 
     pl.semaphore_wait(barrier, n + 1)
     coupled_rows = len(where) * width // n
@@ -257,8 +288,7 @@
 
     share = LANES // n
     pairs = panels // 2
-    inner_rows = halves * 2 * share
-    inner_copies = []
+    inner_rows = halves * panels * share
     for q in range(pairs):
         columns = slice(2 * q * width, 2 * (q + 1) * width)
 
@@ -288,25 +318,19 @@
             for h in range(halves):
                 for k in range(2):
                     source = h * LANES + d * share
-                    target = (d * halves + h) * 2 * share + k * share
-                    inner_part[q, target : target + share, :] = projected[
+                    target = ((d * halves + h) * panels + 2 * q + k) * share
+                    inner_part[target : target + share, :] = projected[
                         source : source + share, k * width : (k + 1) * width
                     ]
-        inner_copies.append(
-            scatter(
-                inner_part.at[q],
-                inner_out.at[q],
-                inner_in.at[q],
-                inner_send.at[0, q],
-                inner_recv.at[0, q],
-                inner_rows,
-            )
-        )
+    inner_copies = scatter(
+        inner_part, inner_out, inner_in, inner_send.at[0], inner_recv.at[0], inner_rows
+    )
     coupled_copies = gather(
         collect(coupled_copies, coupled_part, coupled_in, coupled_rows),
         coupled_all,
         coupled_send.at[1],
         coupled_recv.at[1],
+        ring,
     )
 
     slots_copy.wait()
@@ -329,98 +353,104 @@
                 inner = contract(split(row), split(t_ref[later, later]), PLAIN)
                 t_ref[here, later] = -contract(split(f_ref[k]), split(inner), PLAIN)
 
-    def update(h):
+    def reflect(t):
+        slot = slots_smem[0, t]
+        both = contract((v_high[slot], v_low[slot]), split(t_ref[...]), PLAIN)
+        w_high[t], w_low[t] = split(both)
+
+    def unpack():
         for j in range(n):
-            value = decode(inner_all.at[h, j], panels * share)
-            for k in range(panels):
-                inner[h, j * share : (j + 1) * share, k * width : (k + 1) * width] = value[
-                    k * share : (k + 1) * share, :
-                ]
-        high, low = split(contract(split(t_ref[...]), split(inner[h]), COLUMNS))
-        u_high[:, h * LANES : (h + 1) * LANES] = high
-        u_low[:, h * LANES : (h + 1) * LANES] = low
-
-    def finished(slot, columns):
-        change = contract(
-            (v_high[slot], v_low[slot]), (u_high[:, columns], u_low[:, columns]), PLAIN
-        )
-        value = x_buf[slot, :, columns] - change
-        live = lax.broadcasted_iota(jnp.int32, value.shape, 0) < channels_ref[0, slot]
-        return jnp.where(live, value, 0.0)
+            value = decode(inner_all.at[j], inner_rows)
+            for h in range(halves):
+                for k in range(panels):
+                    source = (h * panels + k) * share
+                    target = h * LANES + j * share
+                    inner[target : target + share, k * width : (k + 1) * width] = value[
+                        source : source + share, :
+                    ]
+
+    def update():
+        u_high[...], u_low[...] = split(contract(split(t_ref[...]), split(inner[...]), COLUMNS))
+
+    def masked(slot, change):
+        live = lax.broadcasted_iota(jnp.int32, (BLOCK, eig), 0) < channels_ref[0, slot]
+        return jnp.where(live, x_buf[slot] - change, 0.0)
 
     kets = {}
 
-    def right_blocks(h):
+    def right_blocks():
         for t in range(tile_slots):
-            ket_out[h, t] = finished(slots_smem[0, t], slice(h * LANES, (h + 1) * LANES)).astype(BF16)
-            copy = pltpu.make_async_remote_copy(
-                src_ref=ket_out.at[h, t],
-                dst_ref=ket_in.at[h, t],
-                send_sem=ket_send.at[h, t],
-                recv_sem=ket_recv.at[h, t],
-                device_id=(before, me),
-                device_id_type=MESH,
-            )
-            copy.start()
-            kets[(h, t)] = copy
+            change = contract((w_high[t], w_low[t]), split(inner[...]), COLUMNS)
+            value = masked(slots_smem[0, t], change).astype(BF16)
+            for h in range(halves):
+                ket_out[h, t] = value[:, h * LANES : (h + 1) * LANES]
+                copy = pltpu.make_async_remote_copy(
+                    src_ref=ket_out.at[h, t],
+                    dst_ref=ket_in.at[h, t],
+                    send_sem=ket_send.at[h, t],
+                    recv_sem=ket_recv.at[h, t],
+                    device_id=(before, me),
+                    device_id_type=MESH,
+                )
+                copy.start()
+                kets[(h, t)] = copy
 
     def left_blocks():
         for t in range(tile_slots):
             occupied = occupied_ref[0, t].astype(F32)
-            bras[t] = (finished(left_ref[0, t], slice(0, eig)) * occupied).astype(BF16)
-
-    totals = [
-        collect(inner_copies[q], inner_part.at[q], inner_in.at[q], inner_rows) for q in range(pairs)
-    ]
-    inner_copies = [
-        gather(
-            jnp.concatenate(
-                [total[h * 2 * share : (h + 1) * 2 * share, :] for total in totals], axis=0
-            ),
-            inner_all.at[h],
-            inner_send.at[1, h],
-            inner_recv.at[1, h],
-        )
-        for h in range(halves)
-    ]
-    for copy in coupled_copies:
-        copy.wait()
+            slot = left_ref[0, t]
+            change = contract((v_high[slot], v_low[slot]), (u_high[...], u_low[...]), PLAIN)
+            bras[t] = (masked(slot, change) * occupied).astype(BF16)
+
+    inner_copies = gather(
+        collect(inner_copies, inner_part, inner_in, inner_rows),
+        inner_all,
+        inner_send.at[1],
+        inner_recv.at[1],
+        ring,
+    )
+    if ring:
+        hand_on(coupled_copies, coupled_all, coupled_send.at[1], coupled_recv.at[1])
+    if ring:
+        hand_on(inner_copies, inner_all, inner_send.at[1], inner_recv.at[1])
+    finish(coupled_copies)
     for j in range(n):
         coupled[j * coupled_rows : (j + 1) * coupled_rows, :] = decode(coupled_all.at[j], coupled_rows)
     transfer_matrix()
     to_smem.wait()
-    for h in range(halves):
-        for copy in inner_copies[h]:
-            copy.wait()
-        update(h)
-        right_blocks(h)
+    for t in range(tile_slots):
+        reflect(t)
+    finish(inner_copies)
+    unpack()
+    right_blocks()
+    update()
     left_blocks()
 
     own_rows = eig // n
     tiles_copy.wait()
     sends = []
-    for h in range(halves):
-        total = jnp.zeros((eig, LANES), F32)
-        for t in range(tile_slots):
+    totals = [jnp.zeros((eig, LANES), F32) for _ in range(halves)]
+    for t in range(tile_slots):
+        for h in range(halves):
             kets[(h, t)].wait()
             product = jnp.dot(tiles_ref[t], ket_in[h, t], preferred_element_type=F32).astype(BF16)
-            total = total + lax.dot_general(
-                bras[t], product, (ROWS, ((), ())), preferred_element_type=F32
-            )
-        own[h] = total.reshape(n, own_rows, LANES)
-        dipole_out[h] = total.reshape(n, own_rows, LANES).astype(BF16)
-        for d in range(1, n):
-            target = lax.rem(me + d, n)
-            copy = pltpu.make_async_remote_copy(
-                src_ref=dipole_out.at[h, target],
-                dst_ref=dipole_in.at[h, d - 1],
-                send_sem=dipole_send.at[h, d - 1],
-                recv_sem=dipole_recv.at[h, d - 1],
-                device_id=(sym, target),
-                device_id_type=MESH,
-            )
-            copy.start()
-            sends.append((h, d, copy))
+            totals[h] = totals[h] + multiply(bras[t], product, ROWS)
+            if t < tile_slots - 1:
+                continue
+            own[h] = totals[h].reshape(n, own_rows, LANES)
+            dipole_out[h] = totals[h].reshape(n, own_rows, LANES).astype(BF16)
+            for d in range(1, n):
+                target = lax.rem(me + d, n)
+                copy = pltpu.make_async_remote_copy(
+                    src_ref=dipole_out.at[h, target],
+                    dst_ref=dipole_in.at[h, d - 1],
+                    send_sem=dipole_send.at[h, d - 1],
+                    recv_sem=dipole_recv.at[h, d - 1],
+                    device_id=(sym, target),
+                    device_id_type=MESH,
+                )
+                copy.start()
+                sends.append((h, d, copy))
     results = [own[h, me] for h in range(halves)]
     for h, d, copy in sends:
         copy.wait()
@@ -451,8 +481,7 @@
     coupled = count * (count - 1) // 2 * width
     coupled_piece = padded(coupled // n) + PACK
     products = len(couplings(count)) * (count // 2) ** 2 * width
-    scatter_piece = padded(2 * eig // n) + PACK
-    inner_piece = padded(count * LANES // n) + PACK
+    inner_piece = padded(count * eig // n) + PACK
     spans = blocks // PROJECT_SPAN
     share = eig // n
     dma = pltpu.SemaphoreType.DMA
@@ -476,13 +505,15 @@
             pltpu.VMEM((n - 1, coupled_piece, LANES), I16),
             pltpu.VMEM((n, coupled_piece, LANES), I16),
             pltpu.VMEM((coupled, LANES), F32),
-            pltpu.VMEM((count // 2, 2 * eig, LANES), F32),
-            pltpu.VMEM((count // 2, n - 1, scatter_piece, LANES), I16),
-            pltpu.VMEM((count // 2, n - 1, scatter_piece, LANES), I16),
-            pltpu.VMEM((halves, n, inner_piece, LANES), I16),
-            pltpu.VMEM((halves, LANES, count * width), F32),
+            pltpu.VMEM((count * eig, LANES), F32),
+            pltpu.VMEM((n - 1, inner_piece, LANES), I16),
+            pltpu.VMEM((n - 1, inner_piece, LANES), I16),
+            pltpu.VMEM((n, inner_piece, LANES), I16),
+            pltpu.VMEM((eig, count * width), F32),
             pltpu.VMEM((spans, 2 * eig, rows // spans), BF16),
             pltpu.VMEM((count * width, count * width), F32),
+            pltpu.VMEM((tile_slots, BLOCK, count * width), BF16),
+            pltpu.VMEM((tile_slots, BLOCK, count * width), BF16),
             pltpu.VMEM((count * width, eig), BF16),
             pltpu.VMEM((count * width, eig), BF16),
             pltpu.VMEM((halves, tile_slots, BLOCK, LANES), BF16),
@@ -499,8 +530,8 @@
             dma((2,)),
             dma((2, n - 1)),
             dma((2, n - 1)),
-            dma((2, max(halves, count // 2), n - 1)),
-            dma((2, max(halves, count // 2), n - 1)),
+            dma((2, n - 1)),
+            dma((2, n - 1)),
             dma((halves, tile_slots)),
             dma((halves, tile_slots)),
             dma((halves, n - 1)),

time: 52 us -> 50.7 us (0.975)
  Pallas kernels: 50.4 us -> 49.1 us
    pallas_call x1, Pallas kernels: 50.4 us -> 49.1 us  [on_device(): pl.pallas_call(functools.partial(kernel, n, syms), out_shape=jax.ShapeDty...]
where the time goes in v5:
time: 50.7 us; the launch traced here: 50.5 us
  Pallas kernels  49.1 us (97%)
  local copies, waits for them, and re-layouts  1.38 us (3%)
    pallas_call x1, Pallas kernels, on_device(): pl.pallas_call(functools.partial(kernel, n, syms), out_shape=jax.ShapeDty...  49.1 us
    unnamed x1, local copies, waits for them, and re-layouts  1.38 us

profile of v5, /device:TPU:1, one launch (start us, length us, event | category | flops | bytes accessed | tf_op | source)
XLA Modules:
  0.0 50.5 jit_solution(4643338893247018498)
XLA Ops:
  0.0 49.1 %shard_map.82 = f32[1,32,256]{2,1,0:T(8,128)} custom-call(f32[8,512,256]{2,1,0:T(8,128)} %bitcast.5, f32[8,512,512]{2,1,0:T(8,128)} %bitcast.4, f32[4,128,128]{2,1,0:T(8,128)} %bitcast.7, bf16[2,512,512]{2,1,0:T(8,128)(2,1)} %bitcast.6, s32[1,2]{1,0:T(1,128)} %right_ref.1, s32[1,2]{1,0:T(1,128)} %left_ref.1, s32[1,2]{1,0:T(1,128)} %occupied_ref.1, ...), custom_call_target="tpu_custom_call" | custom-call | tf_op jit(solution)/shard_map/pallas_call | solution.py:491
  49.1 1.4 %copy.10 = f32[1,32,256]{2,1,0:T(8,128)} copy(f32[1,32,256]{2,1,0:T(8,128)} %shard_map.82) | data formatting | bytes 65536

commit v6 on v5

--- a/solution.py
+++ b/solution.py
@@ -67,12 +67,11 @@
     level = jnp.ceil(jnp.log2(peak) + MARGIN) - TOP
     codes = jnp.round(groups * jnp.exp2(-level)[None])
     target[:rows, :] = codes.reshape(rows, LANES).astype(jnp.int32).astype(I16)
-    both = jnp.concatenate([level, level], axis=0)
-    target[padded(rows) :, :] = both.astype(jnp.int32).astype(I16)
+    target[padded(rows) :, :] = level.astype(jnp.int32).astype(I16)
 
 
 def decode(source, rows):
-    level = source[padded(rows) :, :].astype(jnp.int32).astype(F32)[:8]
+    level = source[padded(rows) :, :].astype(jnp.int32).astype(F32)
     groups = source[:rows, :].astype(jnp.int32).astype(F32).reshape(rows // 8, 8, LANES)
     return (groups * jnp.exp2(level)[None]).reshape(rows, LANES)
 
@@ -479,9 +478,9 @@
     halves = eig // LANES
     blocks = rows // BLOCK
     coupled = count * (count - 1) // 2 * width
-    coupled_piece = padded(coupled // n) + PACK
+    coupled_piece = padded(coupled // n) + 8
     products = len(couplings(count)) * (count // 2) ** 2 * width
-    inner_piece = padded(count * eig // n) + PACK
+    inner_piece = padded(count * eig // n) + 8
     spans = blocks // PROJECT_SPAN
     share = eig // n
     dma = pltpu.SemaphoreType.DMA

time: 50.7 us -> 50.5 us (level)
  no operation moved by 1% of the time
where the time goes in v6:
time: 50.5 us; the launch traced here: 50.3 us
  Pallas kernels  48.9 us (97%)
  local copies, waits for them, and re-layouts  1.38 us (3%)
    pallas_call x1, Pallas kernels, on_device(): pl.pallas_call(functools.partial(kernel, n, syms), out_shape=jax.ShapeDty...  48.9 us
    unnamed x1, local copies, waits for them, and re-layouts  1.38 us

profile of v6, /device:TPU:1, one launch (start us, length us, event | category | flops | bytes accessed | tf_op | source)
XLA Modules:
  0.0 50.3 jit_solution(6728571306047783151)
XLA Ops:
  0.0 48.9 %shard_map.82 = f32[1,32,256]{2,1,0:T(8,128)} custom-call(f32[8,512,256]{2,1,0:T(8,128)} %bitcast.5, f32[8,512,512]{2,1,0:T(8,128)} %bitcast.4, f32[4,128,128]{2,1,0:T(8,128)} %bitcast.7, bf16[2,512,512]{2,1,0:T(8,128)(2,1)} %bitcast.6, s32[1,2]{1,0:T(1,128)} %right_ref.1, s32[1,2]{1,0:T(1,128)} %left_ref.1, s32[1,2]{1,0:T(1,128)} %occupied_ref.1, ...), custom_call_target="tpu_custom_call" | custom-call | tf_op jit(solution)/shard_map/pallas_call | solution.py:490
  48.9 1.4 %copy.10 = f32[1,32,256]{2,1,0:T(8,128)} copy(f32[1,32,256]{2,1,0:T(8,128)} %shard_map.82) | data formatting | bytes 65536

commit v7 on v6

--- a/solution.py
+++ b/solution.py
@@ -222,12 +222,12 @@
         return copy
 
     def scatter(part, outgoing, landing, sends, recvs, rows):
-        copies = []
-        for d in range(1, n):
+        copies = {}
+        for d in sorted(range(1, n), key=lambda d: abs(2 * d - n)):
             peer = lax.rem(me + d, n)
             encode(piece(part, peer, rows), outgoing.at[d - 1])
-            copies.append(send(outgoing.at[d - 1], landing.at[d - 1], sends, recvs, d, peer))
-        return copies
+            copies[d] = send(outgoing.at[d - 1], landing.at[d - 1], sends, recvs, d, peer)
+        return [copies[d] for d in range(1, n)]
 
     def collect(copies, part, landing, rows):
         total = piece(part, me, rows)

time: 50.5 us -> 50 us (0.990)
  no operation moved by 1% of the time
where the time goes in v7:
time: 50 us; the launch traced here: 49.8 us
  Pallas kernels  48.4 us (97%)
  local copies, waits for them, and re-layouts  1.38 us (3%)
    pallas_call x1, Pallas kernels, on_device(): pl.pallas_call(functools.partial(kernel, n, syms), out_shape=jax.ShapeDty...  48.4 us
    unnamed x1, local copies, waits for them, and re-layouts  1.38 us

profile of v7, /device:TPU:1, one launch (start us, length us, event | category | flops | bytes accessed | tf_op | source)
XLA Modules:
  0.0 49.8 jit_solution(15684012089619354255)
XLA Ops:
  0.0 48.4 %shard_map.82 = f32[1,32,256]{2,1,0:T(8,128)} custom-call(f32[8,512,256]{2,1,0:T(8,128)} %bitcast.5, f32[8,512,512]{2,1,0:T(8,128)} %bitcast.4, f32[4,128,128]{2,1,0:T(8,128)} %bitcast.7, bf16[2,512,512]{2,1,0:T(8,128)(2,1)} %bitcast.6, s32[1,2]{1,0:T(1,128)} %right_ref.1, s32[1,2]{1,0:T(1,128)} %left_ref.1, s32[1,2]{1,0:T(1,128)} %occupied_ref.1, ...), custom_call_target="tpu_custom_call" | custom-call | tf_op jit(solution)/shard_map/pallas_call | solution.py:490
  48.4 1.4 %copy.10 = f32[1,32,256]{2,1,0:T(8,128)} copy(f32[1,32,256]{2,1,0:T(8,128)} %shard_map.82) | data formatting | bytes 65536
